TPU v7x, 256 devices: a whole 4x4x8 slice. The times are simulated.
256 devices in a mesh: seq: 8 (over z), bal: 4 (over x), rep: 8 (over y, core).
Axes of the slice: x: 4, y: 4, z: 8, core: 2. Of those that a mesh axis runs over, the one named last changes fastest.
Arguments:
- queries: bfloat16 [32, 6, 512, 2048], P('rep', None, ('seq', 'bal')), parts along dimension 0, may hold values from -16 to 16
- key_tokens: bfloat16 [32, 6, 512, 2048], P('rep', None, ('seq', 'bal')), parts along dimension 0, may hold values from -8 to 8
- value_tokens: bfloat16 [32, 6, 512, 2048], P('rep', None, ('seq', 'bal')), parts along dimension 0, may hold values from -6 to 6
- view_lists: int32 [32, 6, 4], P('rep'), parts along dimension 0, may hold values from -1 to 5, as said below
Outputs:
- attended: bfloat16 [32, 6, 512, 2048], P('rep', None, ('seq', 'bal')), parts along dimension 0
There are 8 independent parts, one for each index of `rep`. A program takes and returns all parts, laid end to end along the dimension named above; each array names one. Nothing has to cross between parts.
Inputs may be any that keep to these rules, and one draw needn't show every extreme that they name: Each list view_lists[w, v] begins with v itself, names distinct views, and holds -1 in every entry after its named views; in every draw some list names 4 views.
All inputs are finite; a program needn't handle non-finite values.
Results may differ from a plain program's by a relative error of at most 0.003.
Values may be sent and summed in bfloat16 or wider, within the bound.
A program may use at most 64 MiB of HBM per device.

v0:
```python
import math

import jax
import jax.numpy as jnp
from jax import lax
from jax.sharding import PartitionSpec as P

HEAD = 128


NEG_FILL = -1e30


def side_by_side(arrays, axis, split_dim, concat_dim, along):
    ends, at = ([], 0)
    for a in arrays[:-1]:
        at += a.shape[along]
        ends.append(at)
    both = jnp.concatenate(arrays, axis=along)
    return tuple(
        jnp.split(
            lax.all_to_all(both, axis, split_axis=split_dim, concat_axis=concat_dim, tiled=True),
            ends,
            axis=along,
        )
    )


def fold_block(carry_state, query_rows, key_rows, value_rows, score_scale):
    row_top, row_total, partial_sum = carry_state
    scores = (
        jnp.einsum("qhd,khd->hqk", query_rows, key_rows, preferred_element_type=jnp.float32)
        * score_scale
    )
    new_top = jnp.maximum(row_top, jnp.max(scores, axis=2))
    rescale = jnp.exp(row_top - new_top)
    exponent = jnp.exp(scores - new_top[:, :, None])
    row_total = row_total * rescale + jnp.sum(exponent, axis=2)
    product = jnp.einsum(
        "hqk,khd->qhd",
        exponent.astype(jnp.bfloat16),
        value_rows,
        preferred_element_type=jnp.float32,
    )
    partial_sum = partial_sum * jnp.transpose(rescale)[:, :, None] + product
    return (new_top, row_total, partial_sum)


def sweep_window(carry_state, query_views, key_views, value_views, window_lists, score_scale):
    tops, totals, sums = carry_state
    new_tops = []
    new_totals = []
    new_sums = []
    for view in range(query_views.shape[0]):
        view_row = window_lists[view]
        list_length = jnp.sum((view_row >= 0).astype(jnp.int32))
        query_rows = query_views[view]

        def advance(slot_index, inner_state):
            key_view = lax.dynamic_index_in_dim(view_row, slot_index, 0, keepdims=False)
            key_rows = lax.dynamic_index_in_dim(key_views, key_view, 0, keepdims=False)
            value_rows = lax.dynamic_index_in_dim(value_views, key_view, 0, keepdims=False)
            return fold_block(inner_state, query_rows, key_rows, value_rows, score_scale)

        result = lax.fori_loop(0, list_length, advance, (tops[view], totals[view], sums[view]))
        new_tops.append(result[0])
        new_totals.append(result[1])
        new_sums.append(result[2])
    return (jnp.stack(new_tops), jnp.stack(new_totals), jnp.stack(new_sums))


def normalize(totals, sums):
    return (sums / jnp.swapaxes(totals, -1, -2)[..., None]).astype(jnp.bfloat16)


def local(queries, key_tokens, value_tokens, view_lists):
    windows, view_count, shard_rows, feature_width = queries.shape
    seq_count = lax.axis_size("seq")
    bal_count = lax.axis_size("bal")
    columns = feature_width // seq_count
    local_heads = columns // HEAD
    score_scale = 1.0 / math.sqrt(HEAD)
    window_rows = seq_count * bal_count * shard_rows

    def joint_form(tokens_in):
        parted = tokens_in.reshape(windows, view_count, shard_rows, seq_count, columns)
        return jnp.transpose(parted, (3, 0, 1, 2, 4)).reshape(
            seq_count * windows, view_count, 1, shard_rows, columns
        )

    exchanged = side_by_side(
        (joint_form(queries), joint_form(key_tokens), joint_form(value_tokens)),
        ("seq", "bal"),
        0,
        2,
        1,
    )
    owned_rows = [
        member.reshape(view_count, window_rows, local_heads, HEAD) for member in exchanged
    ]
    window_lists = lax.dynamic_index_in_dim(view_lists, lax.axis_index("bal"), 0, keepdims=False)
    initial = (
        jnp.full((view_count, local_heads, window_rows), NEG_FILL, jnp.float32),
        jnp.zeros((view_count, local_heads, window_rows), jnp.float32),
        jnp.zeros((view_count, window_rows, local_heads, HEAD), jnp.float32),
    )
    tops, totals, sums = sweep_window(
        initial, owned_rows[0], owned_rows[1], owned_rows[2], window_lists, score_scale
    )
    result = normalize(totals, sums)
    flat_form = result.reshape(1, view_count, seq_count * bal_count, shard_rows, columns)
    returned = lax.all_to_all(flat_form, ("seq", "bal"), split_axis=2, concat_axis=0, tiled=True)
    returned = returned.reshape(seq_count, windows, view_count, shard_rows, columns)
    return jnp.transpose(returned, (1, 2, 3, 0, 4)).reshape(
        windows, view_count, shard_rows, feature_width
    )


def solution(mesh):
    return jax.shard_map(
        local,
        mesh=mesh,
        in_specs=(
            P("rep", None, ("seq", "bal"), None),
            P("rep", None, ("seq", "bal"), None),
            P("rep", None, ("seq", "bal"), None),
            P("rep", None, None),
        ),
        out_specs=P("rep", None, ("seq", "bal"), None),
        check_vma=False,
    )
```

profile of v0, /device:TPU:8, one launch (start us, length us, event | category | flops | bytes accessed | tf_op | source)
XLA Modules:
  0.0 380.7 jit_solution(17612995067881597273)
XLA Ops:
  0.0 1.7 copy.136
  2.1 1.1 copy-done.19
  3.4 2.4 pad_maximum_fusion
  5.8 11.4 %all-to-all-start = ((bf16[32,18,1,16,256]{4,3,1,2,0:T(8,128)(2,1)}), bf16[32,18,1,16,256]{4,3,1,2,0:T(8,128)(2,1)}, u32[]{:S(2)}, u32[]{:S(2)}) async-start(bf16[32,18,1,16,256]{4,3,1,2,0:T(8,128)(2,1)} %pad_maximum_fusion), calls=%async_computation | async-start | bytes 9437184 | tf_op jit(solution)/shard_map/all_to_all | solution.py:22
  19.6 102.8 %all-to-all-done = bf16[32,18,1,16,256]{4,3,1,2,0:T(8,128)(2,1)} async-done(((bf16[32,18,1,16,256]{4,3,1,2,0:T(8,128)(2,1)}), bf16[32,18,1,16,256]{4,3,1,2,0:T(8,128)(2,1)}, u32[]{:S(2)}, u32[]{:S(2)}) %all-to-all-start) | async-done | bytes 4718624 | tf_op jit(solution)/shard_map/all_to_all | solution.py:22
  122.5 3.2 fusion.103
  125.7 2.5 fusion.102
  129.2 1.6 copy.95
  130.7 1.9 reshape.176
  132.6 3.6 copy.98
  136.2 0.9 broadcast.59.clone
  137.0 6.2 %while.84 = (s32[]{:T(128)}, f32[2,512]{1,0:T(2,128)S(1)}, f32[2,512]{1,0:T(2,128)S(1)}, f32[512,2,128]{0,2,1:T(8,128)}, s32[]{:T(128)}, /*index=5*/s32[4]{0:T(1...) while((s32[]{:T(128)}, f32[2,512]{1,0:T(2,128)S(1)}, ...), condition=%wide.region_4.5_spmd, body=%wide.region_1.4_spmd.sunk | while | flops 272894976 | bytes 12386581 | solution.py:65
  141.8 0.8 copy-done.5
  143.3 2.1 copy.99
  145.3 2.3 stack.42
  147.6 1.9 constant_dynamic-update-slice_fusion.5
  149.5 0.8 squeeze.97
  150.2 1.0 copy.101
  151.2 0.9 broadcast.59.clone.1
  152.1 11.4 %while.85 = (s32[]{:T(128)}, f32[2,512]{1,0:T(2,128)S(1)}, f32[2,512]{1,0:T(2,128)S(1)}, f32[512,2,128]{0,2,1:T(8,128)}, s32[]{:T(128)}, /*index=5*/s32[4]{0:T(1...) while((s32[]{:T(128)}, f32[2,512]{1,0:T(2,128)S(1)}, ...), condition=%wide.region_9.10_spmd, body=%wide.region_6.9_spmd.sunk | while | flops 272894976 | bytes 12386581 | solution.py:65
  156.7 0.8 copy-done.7
  162.0 0.8 copy-done.7
  163.5 2.1 copy.103
  165.6 2.3 stack.43
  167.9 0.8 squeeze.99
  168.6 1.0 copy.105
  169.6 0.9 broadcast.59.clone.2
  170.5 5.8 %while.86 = (s32[]{:T(128)}, f32[2,512]{1,0:T(2,128)S(1)}, f32[2,512]{1,0:T(2,128)S(1)}, f32[512,2,128]{0,2,1:T(8,128)}, s32[]{:T(128)}, /*index=5*/s32[4]{0:T(1...) while((s32[]{:T(128)}, f32[2,512]{1,0:T(2,128)S(1)}, ...), condition=%wide.region_14.15_spmd, body=%wide.region_11.14_spmd.sunk | while | flops 272894976 | bytes 12386581 | solution.py:65
  174.9 0.8 copy-done.9
  176.3 2.1 copy.107
  178.4 2.3 stack.44
  180.7 0.8 squeeze.101
  181.4 1.0 copy.109
  182.4 0.9 broadcast.59.clone.3
  183.3 6.2 %while.87 = (s32[]{:T(128)}, f32[2,512]{1,0:T(2,128)S(1)}, f32[2,512]{1,0:T(2,128)S(1)}, f32[512,2,128]{0,2,1:T(8,128)}, s32[]{:T(128)}, /*index=5*/s32[4]{0:T(1...) while((s32[]{:T(128)}, f32[2,512]{1,0:T(2,128)S(1)}, ...), condition=%wide.region_19.20_spmd, body=%wide.region_16.19_spmd.sunk | while | flops 272894976 | bytes 12386581 | solution.py:65
  188.1 0.8 copy-done.11
  189.6 2.1 copy.111
  191.6 2.2 stack.45
  193.9 0.8 squeeze.103
  194.7 1.0 copy.113
  195.7 0.9 broadcast.59.clone.4
  196.5 11.9 %while.88 = (s32[]{:T(128)}, f32[2,512]{1,0:T(2,128)S(1)}, f32[2,512]{1,0:T(2,128)S(1)}, f32[512,2,128]{0,2,1:T(8,128)}, s32[]{:T(128)}, /*index=5*/s32[4]{0:T(1...) while((s32[]{:T(128)}, f32[2,512]{1,0:T(2,128)S(1)}, ...), condition=%wide.region_24.25_spmd, body=%wide.region_21.24_spmd.sunk | while | flops 272894976 | bytes 12386581 | solution.py:65
  201.5 0.8 copy-done.13
  207.0 0.8 copy-done.13
  208.5 2.1 copy.115
  210.6 2.3 stack.46
  212.8 0.8 squeeze.105
  213.6 1.0 copy.117
  214.6 0.9 broadcast.59.clone.5
  215.5 6.0 %while.89 = (s32[]{:T(128)}, f32[2,512]{1,0:T(2,128)S(1)}, f32[2,512]{1,0:T(2,128)S(1)}, f32[512,2,128]{0,2,1:T(8,128)}, s32[]{:T(128)}, /*index=5*/s32[4]{0:T(1...) while((s32[]{:T(128)}, f32[2,512]{1,0:T(2,128)S(1)}, ...), condition=%wide.region_29.30_spmd, body=%wide.region_26.29_spmd.sunk | while | flops 272894976 | bytes 12386581 | solution.py:65
  220.1 0.8 copy-done.3
  221.5 1.3 copy.119
  222.8 1.3 stack.47
  224.1 1.7 copy.120
  225.7 6.2 %div.17 = f32[6,512,2,128]{3,2,1,0:T(2,128)S(1)} broadcast(f32[6,512,2]{2,1,0:T(8,128)} %copy.120), dimensions={0,1,2} | broadcast | bytes 3170304 | tf_op jit(solution)/shard_map/div | solution.py:73
  232.0 3.7 div.18
  235.7 2.0 constant_dynamic-update-slice_fusion.4
  237.7 2.0 constant_dynamic-update-slice_fusion.3
  239.7 0.8 constant_dynamic-update-slice_fusion.2
  240.6 0.8 constant_dynamic-update-slice_fusion.1
  241.4 0.8 constant_dynamic-update-slice_fusion
  242.2 2.5 divide_convert_fusion
  245.0 134.3 %all_to_all.33 = bf16[1,6,32,16,256]{4,3,1,0,2:T(8,128)(2,1)S(1)} all-to-all(bf16[1,6,32,16,256]{4,3,1,0,2:T(8,128)(2,1)S(1)} %copy.121), channel_id=1, replica_groups=mesh['seq'=8,'bal'=4,'rep'=8] {'seq','bal'}, dimensions={2} | all-to-all | bytes 3145728 | tf_op jit(solution)/shard_map/all_to_all | solution.py:112
  379.4 1.3 copy.132
  (136 shorter events, 21.8 us)
Async XLA Ops:
  0.0 17.3 %copy-start = (s32[4,6,4]{1,2,0:T(4,128)S(1)}, s32[4,6,4]{1,2,0:T(4,128)}, u32[]{:S(2)}) copy-start(s32[4,6,4]{1,2,0:T(4,128)} %param.19) | copy-start | bytes 1156
  0.0 1.9 copy-start.18
  1.7 1.5 copy-start.19
  5.8 116.7 %all-to-all-start = ((bf16[32,18,1,16,256]{4,3,1,2,0:T(8,128)(2,1)}), bf16[32,18,1,16,256]{4,3,1,2,0:T(8,128)(2,1)}, u32[]{:S(2)}, u32[]{:S(2)}) async-start(bf16[32,18,1,16,256]{4,3,1,2,0:T(8,128)(2,1)} %pad_maximum_fusion), calls=%async_computation | async-start | bytes 9437184 | tf_op jit(solution)/shard_map/all_to_all | solution.py:22
  140.1 1.0 copy-start.4
  141.8 0.8 copy-start.5
  143.2 6.2 %copy-start.24 = (bf16[1,1,32,16,256]{4,3,1,2,0:T(8,128)(2,1)S(1)}, bf16[1,1,32,16,256]{4,3,1,2,0:T(8,128)(2,1)}, u32[]{:S(2)}) copy-start(bf16[1,1,32,16,256]{4,3,1,2,0:T(8,128)(2,1)} %get-tuple-element.615) | copy-start | bytes 786436
  155.0 1.0 copy-start.6
  156.6 0.8 copy-start.7
  160.3 1.0 copy-start.6
  162.0 0.8 copy-start.7
  163.5 4.4 %copy-start.23 = (bf16[1,1,32,16,256]{4,3,1,2,0:T(8,128)(2,1)S(1)}, bf16[1,1,32,16,256]{4,3,1,2,0:T(8,128)(2,1)}, u32[]{:S(2)}) copy-start(bf16[1,1,32,16,256]{4,3,1,2,0:T(8,128)(2,1)} %get-tuple-element.614) | copy-start | bytes 786436
  173.3 1.0 copy-start.8
  174.9 0.8 copy-start.9
  176.3 4.4 %copy-start.22 = (bf16[1,1,32,16,256]{4,3,1,2,0:T(8,128)(2,1)S(1)}, bf16[1,1,32,16,256]{4,3,1,2,0:T(8,128)(2,1)}, u32[]{:S(2)}) copy-start(bf16[1,1,32,16,256]{4,3,1,2,0:T(8,128)(2,1)} %get-tuple-element.613) | copy-start | bytes 786436
  186.5 1.0 copy-start.10
  188.1 0.8 copy-start.11
  189.6 4.3 %copy-start.21 = (bf16[1,1,32,16,256]{4,3,1,2,0:T(8,128)(2,1)S(1)}, bf16[1,1,32,16,256]{4,3,1,2,0:T(8,128)(2,1)}, u32[]{:S(2)}) copy-start(bf16[1,1,32,16,256]{4,3,1,2,0:T(8,128)(2,1)} %get-tuple-element.612) | copy-start | bytes 786436
  199.8 1.0 copy-start.12
  201.5 0.8 copy-start.13
  205.4 1.0 copy-start.12
  207.0 0.8 copy-start.13
  208.5 4.4 %copy-start.20 = (bf16[1,1,32,16,256]{4,3,1,2,0:T(8,128)(2,1)S(1)}, bf16[1,1,32,16,256]{4,3,1,2,0:T(8,128)(2,1)}, u32[]{:S(2)}) copy-start(bf16[1,1,32,16,256]{4,3,1,2,0:T(8,128)(2,1)} %get-tuple-element.611) | copy-start | bytes 786436
  218.4 1.0 copy-start.2
  220.0 0.8 copy-start.3
  235.7 4.1 %copy-start.15 = (f32[1,1,32,16,256]{4,3,2,1,0:T(8,128)S(1)}, f32[1,1,32,16,256]{4,3,2,1,0:T(8,128)}, u32[]{:S(2)}) copy-start(f32[1,1,32,16,256]{4,3,2,1,0:T(8,128)} %stack.45) | copy-start | bytes 1572868
  235.7 4.9 %copy-start.16 = (f32[1,1,32,16,256]{4,3,2,1,0:T(8,128)S(1)}, f32[1,1,32,16,256]{4,3,2,1,0:T(8,128)}, u32[]{:S(2)}) copy-start(f32[1,1,32,16,256]{4,3,2,1,0:T(8,128)} %stack.46) | copy-start | bytes 1572868
  235.7 5.7 %copy-start.17 = (f32[1,1,32,16,256]{4,3,2,1,0:T(8,128)S(1)}, f32[1,1,32,16,256]{4,3,2,1,0:T(8,128)}, u32[]{:S(2)}) copy-start(f32[1,1,32,16,256]{4,3,2,1,0:T(8,128)} %stack.47) | copy-start | bytes 1572868
  237.7 4.6 %copy-start.14 = (f32[1,6,32,16,256]{4,3,2,1,0:T(8,128)S(1)}, f32[1,6,32,16,256]{4,3,2,1,0:T(8,128)}, u32[]{:S(2)}) copy-start(f32[1,6,32,16,256]{4,3,2,1,0:T(8,128)} %div.18) | copy-start | bytes 9437188
  245.0 135.7 %copy-start.1 = (s32[4,6,4]{1,2,0:T(4,128)S(1)}, s32[4,6,4]{1,2,0:T(4,128)}, u32[]{:S(2)}) copy-start(s32[4,6,4]{1,2,0:T(4,128)} %param.19) | copy-start | bytes 1156
where the time goes:
time: 385 us; the launch traced here: 381 us
  blocking collectives  134 us (35%)
  waiting for transfers between devices  103 us (27%)
  local copies, waits for them, and re-layouts  89.3 us (23%)
  loops' own time  23.7 us (6%)
  starting transfers between devices  11.4 us (3%)
  other arithmetic  10.2 us (3%)
  matrix products  8.49 us (2%)
    all_to_all x1, blocking collectives, local(): lax.all_to_all(flat_form, ('seq', 'bal'), split_axis=2, concat_axis=0, ti...  134 us
    all_to_all x1, waiting for transfers between devices, side_by_side(): lax.all_to_all(both, axis, split_axis=split_dim, concat_axis=concat_dim,...  103 us
    another operation x6, loops' own time, sweep_window(): lax.fori_loop(0, list_length, advance, (tops[view], totals[view], sums[vi...  23.7 us
    while x14, local copies, waits for them, and re-layouts, sweep_window(): lax.fori_loop(0, list_length, advance, (tops[view], totals[view], sums[vi...  20.4 us
    another operation x8, local copies, waits for them, and re-layouts, sweep_window(): return (jnp.stack(new_tops), jnp.stack(new_totals), jnp.stack(new_sums))  13.4 us
    all_to_all x1, starting transfers between devices, side_by_side(): lax.all_to_all(both, axis, split_axis=split_dim, concat_axis=concat_dim,...  11.4 us
    div x2, local copies, waits for them, and re-layouts, normalize(): return (sums / jnp.swapaxes(totals, -1, -2)[..., None]).astype(jnp.bfloat16)  9.91 us
    unnamed x36, local copies, waits for them, and re-layouts  8.93 us
  transfers between devices with their start and end apart: 1, of which 1 were waited for; matrix products, arithmetic and copies ran while one was open for 1% of the time, Pallas kernels for 0%

commit v1 on v0

v1 whole, which is shorter than its diff:
```python
import functools
import math

import jax
import jax.numpy as jnp
from jax import lax
from jax.experimental import pallas as pl
from jax.experimental.pallas import tpu as pltpu
from jax.sharding import PartitionSpec as P

HEAD = 128
QUERY_BLOCK = 256
MESH = pl.DeviceIdType.MESH
ROWS_BY_ROWS = (((1,), (1,)), ((), ()))
EXP2_SCALE = math.log2(math.e) / math.sqrt(HEAD)


def attend(view_lists, window, view, query_buf, key_buf, value_buf, result_buf):
    slots = view_lists.shape[2]
    rows = query_buf.shape[1]
    entries = [view_lists[window, view, slot] for slot in range(slots)]
    named = [jnp.where(entry >= 0, 1.0, 0.0).astype(jnp.float32) for entry in entries]
    key_views = [jnp.where(entry >= 0, entry, view) for entry in entries]

    def block(index, carry):
        span = pl.ds(pl.multiple_of(index * QUERY_BLOCK, QUERY_BLOCK), QUERY_BLOCK)
        query_rows = query_buf[view, span, :]
        scores = [
            lax.dot_general(query_rows, key_buf[u], ROWS_BY_ROWS, preferred_element_type=jnp.float32)
            for u in key_views
        ]
        top = functools.reduce(jnp.maximum, scores)
        top = jnp.max(top, axis=1, keepdims=True) * EXP2_SCALE
        total = jnp.zeros((QUERY_BLOCK, 1), jnp.float32)
        mixed = jnp.zeros((QUERY_BLOCK, HEAD), jnp.float32)
        for slot, u in enumerate(key_views):
            exponent = jnp.exp2(scores[slot] * EXP2_SCALE - top)
            total += jnp.sum(exponent, axis=1, keepdims=True) * named[slot]
            values = value_buf[u] * named[slot].astype(jnp.bfloat16)
            mixed += jnp.dot(exponent.astype(jnp.bfloat16), values, preferred_element_type=jnp.float32)
        result_buf[view, span, :] = (mixed / total).astype(jnp.bfloat16)
        return carry

    lax.fori_loop(0, rows // QUERY_BLOCK, block, 0)


def kernel(
    seq_count, bal_count,
    view_lists, queries, keys, values,
    out,
    q0, q1, k0, k1, v0, v1, r0, r1,
    send_in, recv_in, send_out, recv_out,
):
    seq, bal = lax.axis_index("seq"), lax.axis_index("bal")
    peers = seq_count * bal_count
    me = seq * bal_count + bal
    shard = queries.shape[2]
    views = queries.shape[1]
    heads = 2
    window_rows = peers * shard

    def place(peer):
        return lax.div(peer, bal_count), lax.rem(peer, bal_count)

    def device(peer):
        peer_seq, peer_bal = place(peer)
        return {"seq": peer_seq, "bal": peer_bal}

    def rows_of(peer):
        return pl.ds(pl.multiple_of(peer * shard, shard), shard)

    def columns_of(peer_seq, head):
        return pl.ds(pl.multiple_of(peer_seq * (heads * HEAD) + head * HEAD, HEAD), HEAD)

    barrier = pltpu.get_barrier_semaphore()

    def greet(offset, carry):
        pl.semaphore_signal(
            barrier, inc=1, device_id=device(lax.rem(me + offset, peers)), device_id_type=MESH
        )
        return carry

    lax.fori_loop(1, peers, greet, 0)
    pl.semaphore_wait(barrier, peers - 1)

    inbound = []
    for head, group in enumerate(((k0, v0, q0), (k1, v1, q1))):
        for kind, (source, landing) in enumerate(zip((keys, values, queries), group)):
            inbound.append((head, 3 * head + kind, source, landing))

    for head, number, source, landing in inbound:

        def send(offset, carry):
            peer = lax.rem(me + offset, peers)
            peer_seq, peer_bal = place(peer)
            pltpu.make_async_remote_copy(
                src_ref=source.at[peer_bal, :, :, columns_of(peer_seq, head)],
                dst_ref=landing.at[:, rows_of(me), :],
                send_sem=send_in.at[number],
                recv_sem=recv_in.at[number],
                device_id=device(peer),
                device_id_type=MESH,
            ).start()
            return carry

        lax.fori_loop(1, peers, send, 0)
        pltpu.make_async_copy(
            source.at[bal, :, :, columns_of(seq, head)], landing.at[:, rows_of(me), :], recv_in.at[number]
        ).start()

    for head, landings, result in ((0, (k0, v0, q0), r0), (1, (k1, v1, q1), r1)):
        for kind, landing in enumerate(landings):
            pltpu.make_async_copy(landing, landing, recv_in.at[3 * head + kind]).wait()

        def one_view(view, carry):
            attend(view_lists, bal, view, landings[2], landings[0], landings[1], result)

            def give_back(offset, inner):
                peer = lax.rem(me + offset, peers)
                pltpu.make_async_remote_copy(
                    src_ref=result.at[view, rows_of(peer), :],
                    dst_ref=out.at[bal, view, :, columns_of(seq, head)],
                    send_sem=send_out,
                    recv_sem=recv_out,
                    device_id=device(peer),
                    device_id_type=MESH,
                ).start()
                return inner

            lax.fori_loop(1, peers, give_back, 0)
            pltpu.make_async_copy(
                result.at[view, rows_of(me), :], out.at[bal, view, :, columns_of(seq, head)], recv_out
            ).start()
            return carry

        lax.fori_loop(0, views, one_view, 0)

    pltpu.make_async_copy(out, out, recv_out).wait()
    for head, number, source, landing in inbound:
        sent = landing.at[:, pl.ds(0, window_rows - shard), :]
        pltpu.make_async_copy(sent, sent, send_in.at[number]).wait()
    for result in (r0, r1):
        sent = result.at[:, pl.ds(0, window_rows - shard), :]
        pltpu.make_async_copy(sent, sent, send_out).wait()


def local(seq_count, bal_count, queries, key_tokens, value_tokens, view_lists):
    windows, views, shard, width = queries.shape
    window_rows = seq_count * bal_count * shard
    head_buffer = pltpu.VMEM((views, window_rows, HEAD), jnp.bfloat16)
    return pl.pallas_call(
        functools.partial(kernel, seq_count, bal_count),
        out_shape=jax.ShapeDtypeStruct(queries.shape, jnp.bfloat16),
        in_specs=[pl.BlockSpec(memory_space=pltpu.SMEM)] + [pl.BlockSpec(memory_space=pl.ANY)] * 3,
        out_specs=pl.BlockSpec(memory_space=pl.ANY),
        scratch_shapes=[head_buffer] * 8
        + [
            pltpu.SemaphoreType.DMA((6,)),
            pltpu.SemaphoreType.DMA((6,)),
            pltpu.SemaphoreType.DMA,
            pltpu.SemaphoreType.DMA,
        ],
        compiler_params=pltpu.CompilerParams(
            collective_id=0, has_side_effects=True, vmem_limit_bytes=48 * 2**20
        ),
    )(view_lists, queries, key_tokens, value_tokens)


def solution(mesh):
    spec = P("rep", None, ("seq", "bal"), None)
    return jax.shard_map(
        functools.partial(local, mesh.shape["seq"], mesh.shape["bal"]),
        mesh=mesh,
        in_specs=(spec, spec, spec, P("rep", None, None)),
        out_specs=spec,
        check_vma=False,
    )
```

time: 385 us -> 153 us (0.40); the launches traced: 381 us -> 153 us
  Pallas kernels: 0 us -> 148 us
  blocking collectives: 134 us -> 0 us
  waiting for transfers between devices: 103 us -> 0 us
  local copies, waits for them, and re-layouts: 89.3 us -> 4.76 us
  loops' own time: 23.7 us -> 0 us
  starting transfers between devices: 11.4 us -> 0 us
  other arithmetic: 10.2 us -> 0 us
  matrix products: 8.49 us -> 0 us
    pallas_call x0 -> x1, Pallas kernels: none -> 148 us  [local(): pl.pallas_call(functools.partial(kernel, seq_count, bal_count), out_shape...]
    all_to_all x1 -> x0, blocking collectives: 134 us -> none  [local(): lax.all_to_all(flat_form, ('seq', 'bal'), split_axis=2, concat_axis=0, ti...]
    all_to_all x1 -> x0, waiting for transfers between devices: 103 us -> none  [side_by_side(): lax.all_to_all(both, axis, split_axis=split_dim, concat_axis=concat_dim,...]
    while x54 -> x0, local copies, waits for them, and re-layouts: 28.1 us -> none  [the longest x14 20.4 us: sweep_window(): lax.fori_loop(0, list_length, advance, (tops[view], totals[view], sums[vi...]
    another operation x6 -> x0, loops' own time: 23.7 us -> none  [sweep_window(): lax.fori_loop(0, list_length, advance, (tops[view], totals[view], sums[vi...]
    another operation x26 -> x0, local copies, waits for them, and re-layouts: 18.6 us -> none  [the longest x8 13.4 us: sweep_window(): return (jnp.stack(new_tops), jnp.stack(new_totals), jnp.stack(new_sums))]
    all_to_all x1 -> x0, starting transfers between devices: 11.4 us -> none  [side_by_side(): lax.all_to_all(both, axis, split_axis=split_dim, concat_axis=concat_dim,...]
    div x2 -> x0, local copies, waits for them, and re-layouts: 9.91 us -> none  [normalize(): return (sums / jnp.swapaxes(totals, -1, -2)[..., None]).astype(jnp.bfloat16)]
  transfers between devices with their start and end apart: 1 -> 0, of which waited for: 1 -> 0; matrix products, arithmetic and copies ran while one was open for 1% -> 0% of each run, Pallas kernels for 0% -> 0%
where the time goes in v1:
time: 153 us
  Pallas kernels  148 us (97%)
  local copies, waits for them, and re-layouts  4.76 us (3%)
    pallas_call x1, Pallas kernels, local(): pl.pallas_call(functools.partial(kernel, seq_count, bal_count), out_shape...  148 us
    unnamed x6, local copies, waits for them, and re-layouts  4.76 us

profile of v1, /device:TPU:8, one launch (start us, length us, event | category | flops | bytes accessed | tf_op | source)
XLA Modules:
  0.0 152.8 jit_solution(16124792767570105507)
XLA Ops:
  0.0 0.8 copy.5.view_lists
  0.8 0.0 copy-start
  0.8 1.4 copy-done
  2.2 0.0 copy-start.1
  2.2 1.4 copy-done.1
  3.6 148.0 %shard_map.46 = bf16[4,6,16,2048]{3,2,1,0:T(8,128)(2,1)S(1)} custom-call(s32[4,6,4]{2,1,0:T(8,128)S(1)} %copy.5.view_lists, bf16[4,6,16,2048]{3,2,1,0:T(8,128)(2,1)S(1)} %copy-done, bf16[4,6,16,2048]{3,2,1,0:T(8,128)(2,1)S(1)} %copy-done.1, bf16[4,6,16,2048]{3,2,1,0:T(8,128)(2,1)} %values.1), custom_call_target="tpu_custom_call" | custom-call | tf_op jit(solution)/shard_map/pallas_call | solution.py:151
  151.6 1.1 copy.7
Async XLA Ops:
  0.8 1.4 copy-start
  2.2 1.4 copy-start.1

commit v2 on v1

--- a/solution.py
+++ b/solution.py
@@ -16,9 +16,9 @@
 
 
 def attend(view_lists, window, view, query_buf, key_buf, value_buf, result_buf):
-    slots = view_lists.shape[2]
+    slots = view_lists.shape[1]
     rows = query_buf.shape[1]
-    entries = [view_lists[window, view, slot] for slot in range(slots)]
+    entries = [view_lists[window, slot, view] for slot in range(slots)]
     named = [jnp.where(entry >= 0, 1.0, 0.0).astype(jnp.float32) for entry in entries]
     key_views = [jnp.where(entry >= 0, entry, view) for entry in entries]
 
@@ -150,9 +150,8 @@
     head_buffer = pltpu.VMEM((views, window_rows, HEAD), jnp.bfloat16)
     return pl.pallas_call(
         functools.partial(kernel, seq_count, bal_count),
-        out_shape=jax.ShapeDtypeStruct(queries.shape, jnp.bfloat16),
+        out_shape=pltpu.VMEM(queries.shape, jnp.bfloat16),
         in_specs=[pl.BlockSpec(memory_space=pltpu.SMEM)] + [pl.BlockSpec(memory_space=pl.ANY)] * 3,
-        out_specs=pl.BlockSpec(memory_space=pl.ANY),
         scratch_shapes=[head_buffer] * 8
         + [
             pltpu.SemaphoreType.DMA((6,)),
@@ -161,9 +160,9 @@
             pltpu.SemaphoreType.DMA,
         ],
         compiler_params=pltpu.CompilerParams(
-            collective_id=0, has_side_effects=True, vmem_limit_bytes=48 * 2**20
+            collective_id=0, has_side_effects=True, vmem_limit_bytes=62 * 2**20
         ),
-    )(view_lists, queries, key_tokens, value_tokens)
+    )(jnp.swapaxes(view_lists, 1, 2), queries, key_tokens, value_tokens)
 
 
 def solution(mesh):

time: 153 us -> 149 us (0.974)
  local copies, waits for them, and re-layouts: 4.76 us -> 1.15 us
    unnamed x6 -> x1, local copies, waits for them, and re-layouts: 4.76 us -> 1.15 us
where the time goes in v2:
time: 149 us
  Pallas kernels  148 us (99%)
    pallas_call x1, Pallas kernels, local(): pl.pallas_call(functools.partial(kernel, seq_count, bal_count), out_shape...  148 us

profile of v2, /device:TPU:8, one launch (start us, length us, event | category | flops | bytes accessed | tf_op | source)
XLA Modules:
  0.0 149.4 jit_solution(12795344412319374241)
XLA Ops:
  0.0 148.2 %shard_map.46 = bf16[4,6,16,2048]{3,2,1,0:T(8,128)(2,1)S(1)} custom-call(s32[4,4,6]{2,1,0:T(4,128)} %bitcast.1, bf16[4,6,16,2048]{3,2,1,0:T(8,128)(2,1)} %queries.1, bf16[4,6,16,2048]{3,2,1,0:T(8,128)(2,1)} %keys.1, bf16[4,6,16,2048]{3,2,1,0:T(8,128)(2,1)} %values.1), custom_call_target="tpu_custom_call" | custom-call | tf_op jit(solution)/shard_map/pallas_call | solution.py:151
  148.2 1.1 copy.6

commit v3 on v2

v3 whole, which is shorter than its diff:
```python
import functools
import math

import jax
import jax.numpy as jnp
from jax import lax
from jax.experimental import pallas as pl
from jax.experimental.pallas import tpu as pltpu
from jax.sharding import PartitionSpec as P

HEAD = 128
QUERY_BLOCK = 256
MESH = pl.DeviceIdType.MESH
ROWS_BY_ROWS = (((1,), (1,)), ((), ()))
EXP2_SCALE = math.log2(math.e) / math.sqrt(HEAD)


def attend(view_lists, window, view, query_buf, key_buf, value_buf, result_buf):
    slots = view_lists.shape[1]
    rows = query_buf.shape[1]
    entries = [view_lists[window, slot, view] for slot in range(slots)]
    named = [jnp.where(entry >= 0, 1.0, 0.0).astype(jnp.float32) for entry in entries]
    key_views = [jnp.where(entry >= 0, entry, view) for entry in entries]

    def block(index, carry):
        span = pl.ds(pl.multiple_of(index * QUERY_BLOCK, QUERY_BLOCK), QUERY_BLOCK)
        query_rows = query_buf[view, span, :]
        scores = [
            lax.dot_general(query_rows, key_buf[u], ROWS_BY_ROWS, preferred_element_type=jnp.float32)
            for u in key_views
        ]
        top = functools.reduce(jnp.maximum, scores)
        top = jnp.max(top, axis=1, keepdims=True) * EXP2_SCALE
        total = jnp.zeros((QUERY_BLOCK, 1), jnp.float32)
        mixed = jnp.zeros((QUERY_BLOCK, HEAD), jnp.float32)
        for slot, u in enumerate(key_views):
            exponent = jnp.exp2(scores[slot] * EXP2_SCALE - top)
            total += jnp.sum(exponent, axis=1, keepdims=True) * named[slot]
            values = value_buf[u] * named[slot].astype(jnp.bfloat16)
            mixed += jnp.dot(exponent.astype(jnp.bfloat16), values, preferred_element_type=jnp.float32)
        result_buf[view, span, :] = (mixed / total).astype(jnp.bfloat16)
        return carry

    lax.fori_loop(0, rows // QUERY_BLOCK, block, 0)


def kernel(
    seq_count, bal_count,
    lists_in, queries, keys, values,
    out,
    q0, q1, k0, k1, v0, v1, r0, r1,
    send_in, recv_in, send_out, recv_out, columns_in,
    view_lists, lists_sem,
):
    seq, bal = lax.axis_index("seq"), lax.axis_index("bal")
    peers = seq_count * bal_count
    me = seq * bal_count + bal
    shard = queries.shape[2]
    views = queries.shape[1]
    heads = 2
    window_rows = peers * shard

    def loop(first, last, body):
        def run(index, carry):
            body(index)
            return carry

        lax.fori_loop(first, last, run, 0)

    def at(along_seq, along_bal):
        return lax.rem(seq + along_seq, seq_count), lax.rem(bal + along_bal, bal_count)

    def device(peer):
        return {"seq": peer[0], "bal": peer[1]}

    def rows_of(number):
        return pl.ds(pl.multiple_of(number * shard, shard), shard)

    def columns_of(peer_seq, head):
        return pl.ds(pl.multiple_of(peer_seq * (heads * HEAD) + head * HEAD, HEAD), HEAD)

    def greet(semaphore, along_seq, along_bal):
        peer = at(along_seq, along_bal)
        pl.semaphore_signal(semaphore, inc=1, device_id=device(peer), device_id_type=MESH)

    everything, early, late = (0, views), (0, views // 2), (views // 2, views - views // 2)
    inbound = []
    for head, source, landing, part in (
        (0, keys, k0, everything),
        (0, values, v0, everything),
        (0, queries, q0, everything),
        (1, keys, k1, everything),
        (1, values, v1, everything),
        (1, queries, q1, early),
        (1, queries, q1, late),
    ):
        inbound.append((head, len(inbound), source, landing, pl.ds(*part)))

    def send(piece, along_seq, along_bal):
        head, number, source, landing, part = piece
        peer = at(along_seq, along_bal)
        pltpu.make_async_remote_copy(
            src_ref=source.at[peer[1], part, :, columns_of(peer[0], head)],
            dst_ref=landing.at[part, rows_of(me), :],
            send_sem=send_in.at[number],
            recv_sem=recv_in.at[number],
            device_id=device(peer),
            device_id_type=MESH,
        ).start()

    def keep(piece):
        head, number, source, landing, part = piece
        pltpu.make_async_copy(
            source.at[bal, part, :, columns_of(seq, head)], landing.at[part, rows_of(me), :], recv_in.at[number]
        ).start()

    lists = pltpu.make_async_copy(lists_in, view_lists, lists_sem)
    lists.start()

    barrier = pltpu.get_barrier_semaphore()
    loop(1, seq_count, lambda dz: greet(barrier, dz, 0))
    loop(1, bal_count, lambda dx: greet(barrier, 0, dx))
    pl.semaphore_wait(barrier, seq_count + bal_count - 2)
    loop(1, bal_count, lambda dx: greet(columns_in, 0, dx))
    loop(1, seq_count, lambda dz: send(inbound[0], dz, 0))
    loop(1, bal_count, lambda dx: send(inbound[0], 0, dx))
    keep(inbound[0])
    pl.semaphore_wait(columns_in, bal_count - 1)

    loop(1, seq_count, lambda dz: loop(1, bal_count, lambda dx: send(inbound[0], dz, dx)))
    for piece in inbound[1:]:
        loop(1, peers, lambda step: send(piece, lax.div(step, bal_count), lax.rem(step, bal_count)))
        keep(piece)

    def arrive(piece):
        head, number, source, landing, part = piece
        whole = landing.at[part]
        pltpu.make_async_copy(whole, whole, recv_in.at[number]).wait()

    def give_back(head, result, view):
        def give(step):
            other = jnp.where(step - 1 >= me, step, step - 1)
            peer = lax.div(other, bal_count), lax.rem(other, bal_count)
            pltpu.make_async_remote_copy(
                src_ref=result.at[view, rows_of(peer[0] * bal_count + peer[1]), :],
                dst_ref=out.at[bal, view, :, columns_of(seq, head)],
                send_sem=send_out,
                recv_sem=recv_out,
                device_id=device(peer),
                device_id_type=MESH,
            ).start()

        loop(1, peers, give)
        pltpu.make_async_copy(
            result.at[view, rows_of(me), :], out.at[bal, view, :, columns_of(seq, head)], recv_out
        ).start()

    for piece in inbound[:3]:
        arrive(piece)

    lists.wait()

    def first_head(view):
        attend(view_lists, bal, view, q0, k0, v0, r0)
        give_back(0, r0, view)

    loop(0, views, first_head)
    for piece in inbound[3:6]:
        arrive(piece)

    def second_head(view):
        attend(view_lists, bal, view, q1, k1, v1, r1)
        give_back(1, r1, view)

    loop(0, early[1], second_head)
    arrive(inbound[6])
    loop(early[1], views, second_head)

    pltpu.make_async_copy(out, out, recv_out).wait()
    for head, number, source, landing, part in inbound:
        sent = landing.at[part, pl.ds(0, window_rows - shard), :]
        pltpu.make_async_copy(sent, sent, send_in.at[number]).wait()
    for result in (r0, r1):
        sent = result.at[:, pl.ds(0, window_rows - shard), :]
        pltpu.make_async_copy(sent, sent, send_out).wait()


def local(seq_count, bal_count, queries, key_tokens, value_tokens, view_lists):
    windows, views, shard, width = queries.shape
    window_rows = seq_count * bal_count * shard
    head_buffer = pltpu.VMEM((views, window_rows, HEAD), jnp.bfloat16)
    return pl.pallas_call(
        functools.partial(kernel, seq_count, bal_count),
        out_shape=pltpu.VMEM(queries.shape, jnp.bfloat16),
        in_specs=[pl.BlockSpec(memory_space=pl.ANY)] * 4,
        scratch_shapes=[head_buffer] * 8
        + [
            pltpu.SemaphoreType.DMA((7,)),
            pltpu.SemaphoreType.DMA((7,)),
            pltpu.SemaphoreType.DMA,
            pltpu.SemaphoreType.DMA,
            pltpu.SemaphoreType.REGULAR,
            pltpu.SMEM((windows, view_lists.shape[2], views), jnp.int32),
            pltpu.SemaphoreType.DMA,
        ],
        compiler_params=pltpu.CompilerParams(
            collective_id=0, has_side_effects=True, vmem_limit_bytes=62 * 2**20
        ),
    )(jnp.swapaxes(view_lists, 1, 2), queries, key_tokens, value_tokens)


def solution(mesh):
    spec = P("rep", None, ("seq", "bal"), None)
    return jax.shard_map(
        functools.partial(local, mesh.shape["seq"], mesh.shape["bal"]),
        mesh=mesh,
        in_specs=(spec, spec, spec, P("rep", None, None)),
        out_specs=spec,
        check_vma=False,
    )
```

time: 149 us -> 147 us (0.987)
  Pallas kernels: 148 us -> 145 us
    pallas_call x1, Pallas kernels: 148 us -> 145 us  [local(): pl.pallas_call(functools.partial(kernel, seq_count, bal_count), out_shape...]
where the time goes in v3:
time: 147 us
  Pallas kernels  145 us (99%)
    pallas_call x1, Pallas kernels, local(): pl.pallas_call(functools.partial(kernel, seq_count, bal_count), out_shape...  145 us

profile of v3, /device:TPU:8, one launch (start us, length us, event | category | flops | bytes accessed | tf_op | source)
XLA Modules:
  0.0 146.5 jit_solution(4682374552224447069)
XLA Ops:
  0.0 145.4 %shard_map.46 = bf16[4,6,16,2048]{3,2,1,0:T(8,128)(2,1)S(1)} custom-call(s32[4,4,6]{2,1,0:T(4,128)} %bitcast.1, bf16[4,6,16,2048]{3,2,1,0:T(8,128)(2,1)} %queries.1, bf16[4,6,16,2048]{3,2,1,0:T(8,128)(2,1)} %keys.1, bf16[4,6,16,2048]{3,2,1,0:T(8,128)(2,1)} %values.1), custom_call_target="tpu_custom_call" | custom-call | tf_op jit(solution)/shard_map/pallas_call | solution.py:192
  145.4 1.1 copy.6

commit v4 on v3

--- a/solution.py
+++ b/solution.py
@@ -46,12 +46,19 @@
 
 def kernel(
     seq_count, bal_count,
-    lists_in, queries, keys, values,
+    lists_in, queries_in, keys_in, values_in,
     out,
     q0, q1, k0, k1, v0, v1, r0, r1,
     send_in, recv_in, send_out, recv_out, columns_in,
-    view_lists, lists_sem,
+    view_lists, lists_sem, queries, keys, values, staged,
 ):
+    stages = [
+        pltpu.make_async_copy(given, copy, staged.at[number])
+        for number, (given, copy) in enumerate(((keys_in, keys), (values_in, values), (queries_in, queries)))
+    ]
+    for stage in stages:
+        stage.start()
+
     seq, bal = lax.axis_index("seq"), lax.axis_index("bal")
     peers = seq_count * bal_count
     me = seq * bal_count + bal
@@ -122,6 +129,7 @@
     loop(1, bal_count, lambda dx: greet(barrier, 0, dx))
     pl.semaphore_wait(barrier, seq_count + bal_count - 2)
     loop(1, bal_count, lambda dx: greet(columns_in, 0, dx))
+    stages[0].wait()
     loop(1, seq_count, lambda dz: send(inbound[0], dz, 0))
     loop(1, bal_count, lambda dx: send(inbound[0], 0, dx))
     keep(inbound[0])
@@ -129,6 +137,8 @@
 
     loop(1, seq_count, lambda dz: loop(1, bal_count, lambda dx: send(inbound[0], dz, dx)))
     for piece in inbound[1:]:
+        if piece[1] < len(stages):
+            stages[piece[1]].wait()
         loop(1, peers, lambda step: send(piece, lax.div(step, bal_count), lax.rem(step, bal_count)))
         keep(piece)
 
@@ -139,7 +149,10 @@
 
     def give_back(head, result, view):
         def give(step):
-            other = jnp.where(step - 1 >= me, step, step - 1)
+            half = peers // 2
+            low = jnp.where(step - 1 >= me, step, step - 1)
+            high = half + lax.rem(me + step - half, half)
+            other = jnp.where(step < half + jnp.where(me >= half, 1, 0), low, high)
             peer = lax.div(other, bal_count), lax.rem(other, bal_count)
             pltpu.make_async_remote_copy(
                 src_ref=result.at[view, rows_of(peer[0] * bal_count + peer[1]), :],
@@ -202,6 +215,10 @@
             pltpu.SemaphoreType.REGULAR,
             pltpu.SMEM((windows, view_lists.shape[2], views), jnp.int32),
             pltpu.SemaphoreType.DMA,
+        ]
+        + [pltpu.VMEM(queries.shape, jnp.bfloat16)] * 3
+        + [
+            pltpu.SemaphoreType.DMA((3,)),
         ],
         compiler_params=pltpu.CompilerParams(
             collective_id=0, has_side_effects=True, vmem_limit_bytes=62 * 2**20

time: 147 us -> 147 us (level)
  no operation moved by 1% of the time
where the time goes in v4:
time: 147 us; the launch traced here: 146 us
  Pallas kernels  145 us (99%)
    pallas_call x1, Pallas kernels, local(): pl.pallas_call(functools.partial(kernel, seq_count, bal_count), out_shape...  145 us

profile of v4, /device:TPU:8, one launch (start us, length us, event | category | flops | bytes accessed | tf_op | source)
XLA Modules:
  0.0 146.5 jit_solution(6670433680865394621)
XLA Ops:
  0.0 145.3 %shard_map.46 = bf16[4,6,16,2048]{3,2,1,0:T(8,128)(2,1)S(1)} custom-call(s32[4,4,6]{2,1,0:T(4,128)} %bitcast.1, bf16[4,6,16,2048]{3,2,1,0:T(8,128)(2,1)} %queries_in.1, bf16[4,6,16,2048]{3,2,1,0:T(8,128)(2,1)} %keys_in.1, bf16[4,6,16,2048]{3,2,1,0:T(8,128)(2,1)} %values_in.1), custom_call_target="tpu_custom_call" | custom-call | tf_op jit(solution)/shard_map/pallas_call | solution.py:205
  145.3 1.1 copy.6

commit v5 on v4

--- a/solution.py
+++ b/solution.py
@@ -49,7 +49,7 @@
     lists_in, queries_in, keys_in, values_in,
     out,
     q0, q1, k0, k1, v0, v1, r0, r1,
-    send_in, recv_in, send_out, recv_out, columns_in,
+    send_in, recv_in, send_out, recv_out, columns_in, near_in, far_in,
     view_lists, lists_sem, queries, keys, values, staged,
 ):
     stages = [
@@ -124,18 +124,38 @@
     lists = pltpu.make_async_copy(lists_in, view_lists, lists_sem)
     lists.start()
 
+    first = inbound[0]
+    far = seq_count // 2
+
+    def both(distance, body):
+        body(distance)
+        body(seq_count - distance)
+
+    def row(dz):
+        loop(1, bal_count, lambda dx: send(first, dz, dx))
+
     barrier = pltpu.get_barrier_semaphore()
-    loop(1, seq_count, lambda dz: greet(barrier, dz, 0))
+    both(1, lambda dz: greet(barrier, dz, 0))
     loop(1, bal_count, lambda dx: greet(barrier, 0, dx))
-    pl.semaphore_wait(barrier, seq_count + bal_count - 2)
+    pl.semaphore_wait(barrier, bal_count + 1)
+    both(1, lambda dz: greet(near_in, dz, 0))
+    stages[0].wait()
+    both(1, lambda dz: send(first, dz, 0))
+    row(0)
+    keep(first)
+    pl.semaphore_wait(near_in, 2)
+    both(2, lambda dz: greet(far_in, dz, 0))
+    both(2, lambda dz: send(first, dz, 0))
+    both(1, row)
+    pl.semaphore_wait(far_in, 2)
     loop(1, bal_count, lambda dx: greet(columns_in, 0, dx))
-    stages[0].wait()
-    loop(1, seq_count, lambda dz: send(inbound[0], dz, 0))
-    loop(1, bal_count, lambda dx: send(inbound[0], 0, dx))
-    keep(inbound[0])
+    both(3, lambda dz: send(first, dz, 0))
+    send(first, far, 0)
+    both(2, row)
+    both(3, row)
     pl.semaphore_wait(columns_in, bal_count - 1)
-
-    loop(1, seq_count, lambda dz: loop(1, bal_count, lambda dx: send(inbound[0], dz, dx)))
+    row(far)
+
     for piece in inbound[1:]:
         if piece[1] < len(stages):
             stages[piece[1]].wait()
@@ -213,6 +233,8 @@
             pltpu.SemaphoreType.DMA,
             pltpu.SemaphoreType.DMA,
             pltpu.SemaphoreType.REGULAR,
+            pltpu.SemaphoreType.REGULAR,
+            pltpu.SemaphoreType.REGULAR,
             pltpu.SMEM((windows, view_lists.shape[2], views), jnp.int32),
             pltpu.SemaphoreType.DMA,
         ]

time: 147 us -> 147 us (level)
  no operation moved by 1% of the time
where the time goes in v5:
time: 147 us; the launch traced here: 146 us
  Pallas kernels  145 us (99%)
    pallas_call x1, Pallas kernels, local(): pl.pallas_call(functools.partial(kernel, seq_count, bal_count), out_shape...  145 us

profile of v5, /device:TPU:8, one launch (start us, length us, event | category | flops | bytes accessed | tf_op | source)
XLA Modules:
  0.0 146.5 jit_solution(9686278111398826027)
XLA Ops:
  0.0 145.3 %shard_map.46 = bf16[4,6,16,2048]{3,2,1,0:T(8,128)(2,1)S(1)} custom-call(s32[4,4,6]{2,1,0:T(4,128)} %bitcast.1, bf16[4,6,16,2048]{3,2,1,0:T(8,128)(2,1)} %queries_in.1, bf16[4,6,16,2048]{3,2,1,0:T(8,128)(2,1)} %keys_in.1, bf16[4,6,16,2048]{3,2,1,0:T(8,128)(2,1)} %values_in.1), custom_call_target="tpu_custom_call" | custom-call | tf_op jit(solution)/shard_map/pallas_call | solution.py:225
  145.3 1.1 copy.6
